TPU v7x, 512 devices: a whole 4x4x16 slice. The times are simulated.
512 devices in a mesh: root: 4 (over z_hi, core), col: 128 (over z_lo, y, x).
Axes of the slice: x: 4, y: 4, z: 16 (z_hi: 2, z_lo: 8; z = z_hi * 8 + z_lo), core: 2. Of those that a mesh axis runs over, the one named last changes fastest.
Arguments:
- coeffs: float32 [4, 3072, 3072], P('root', 'col'), may hold values from -6 to 6
- diagonal: float32 [3072, 3072], P('col'), may hold values from -1 to 1
- shift: float32 [4], P('root'), may hold values from -1 to 1
- rotation: float32 [4, 4], replicated, may hold values from -1 to 1, as said below
- string_blocks: bfloat16 [30720, 128], P('col'), may hold values from -0.15625 to 0.15625
- block_cols: int32 [24, 10], replicated, may hold values from 0 to 23, all different within a row
Outputs:
- filtered: float32 [4, 3072, 3072], P('root', 'col')
Inputs may be any that keep to these rules, and one draw needn't show every extreme that they name: `block_cols`: each row names 10 different block columns, and every block column is named by some row. rotation is an orthogonal matrix.
All inputs are finite; a program needn't handle non-finite values.
Results may differ from a plain program's by a relative error of at most 0.0003.
Values may be sent and summed in bfloat16 or wider, within the bound.
A program may use at most 64 MiB of HBM per device.

v0:
```python
import jax
import jax.numpy as jnp
from jax import lax
from jax.sharding import PartitionSpec as P


def apply_blocks(matrix, operator_blocks, block_cols):
    height, breadth = matrix.shape
    nblocks, filled = block_cols.shape
    blocksize = breadth // nblocks
    grouped = matrix.reshape(height, nblocks, blocksize)
    picked = jnp.take(grouped, block_cols, axis=1)
    tiles = operator_blocks.reshape(nblocks, filled, blocksize, blocksize).astype(jnp.float32)
    result = jnp.einsum("rifk,ifjk->rij", picked, tiles, precision=lax.Precision.HIGHEST)
    return result.reshape(height, breadth)


def layout_pieces(stacked):
    count, height, breadth = stacked.shape
    groups = breadth // height
    return (
        stacked.reshape(count, height, groups, height)
        .transpose(0, 2, 1, 3)
        .reshape(count, groups, height * height)
    )


def layout_whole(moved, height):
    count = moved.shape[0]
    groups = moved.shape[1]
    return (
        moved.reshape(count, groups, height, height)
        .transpose(0, 3, 1, 2)
        .reshape(count, height, groups * height)
    )


def swap_layout(stacked):
    moved = lax.all_to_all(layout_pieces(stacked), "col", split_axis=1, concat_axis=1, tiled=True)
    return layout_whole(moved, stacked.shape[1])


def shards(coeffs, diagonal, shift, rotation, string_blocks, block_cols):
    start = coeffs[0]
    energy = shift[0]
    operator_blocks = lax.all_gather(string_blocks, "col", axis=0, tiled=True)

    def apply_local(matrix):
        return apply_blocks(matrix, operator_blocks, block_cols)

    def sigma_local(vector):
        turned = swap_layout(vector[None])[0]
        beta_turned = apply_local(turned)
        beta_part = swap_layout(beta_turned[None])[0]
        return apply_local(vector) + beta_part + diagonal * vector

    first = 0.5 * (sigma_local(start) - energy * start)
    second = sigma_local(first) - energy * first - start
    all_roots = lax.all_gather(second[None], "root", axis=0, tiled=True)
    weights = lax.dynamic_index_in_dim(rotation, lax.axis_index("root"), 0, keepdims=False)
    result = jnp.einsum("s,sba->ba", weights, all_roots, precision=lax.Precision.HIGHEST)
    return result[None]


def solution(mesh):
    return jax.shard_map(
        shards,
        mesh=mesh,
        in_specs=(P("root", "col", None), P("col", None), P("root"), P(), P("col", None), P()),
        out_specs=P("root", "col", None),
        check_vma=False,
    )
```

profile of v0, /device:TPU:1, one launch (start us, length us, event | category | flops | bytes accessed | tf_op | source)
XLA Modules:
  0.0 1165.1 jit_solution(13638159206079844193)
XLA Ops:
  6.5 0.7 all-gather.4.cloned.1.call-update
  7.3 2.1 reshape_broadcast_in_dim_squeeze.3
  9.4 0.4 copy.61
  9.8 1.0 copy.62
  10.8 20.4 %all-to-all-start = ((f32[1,128,576]{2,0,1:T(1,128)}), f32[1,128,576]{2,0,1:T(1,128)S(1)}, u32[]{:S(2)}, u32[]{:S(2)}) async-start(f32[1,128,576]{2,0,1:T(1,128)} %copy.62), calls=%async_computation | async-start | bytes 655360 | tf_op jit(solution)/shard_map/all_to_all | solution.py:39
  31.5 21.5 %all-to-all-done = f32[1,128,576]{2,0,1:T(1,128)S(1)} async-done(((f32[1,128,576]{2,0,1:T(1,128)}), f32[1,128,576]{2,0,1:T(1,128)S(1)}, u32[]{:S(2)}, u32[]{:S(2)}) %all-to-all-start) | async-done | bytes 294944 | tf_op jit(solution)/shard_map/all_to_all | solution.py:39
  52.9 0.2 copy.63
  53.1 0.5 copy.64
  53.6 0.9 reshape_squeeze_reshape.6
  54.6 1.0 gather_fusion.1
  55.6 841.9 %all-gather.4.cloned.1.call-done = bf16[30720,128]{1,0:T(8,128)(2,1)} async-done(((bf16[240,128]{1,0:T(8,128)(2,1)}), bf16[30720,128]{1,0:T(8,128)(2,1)}) %all-gather.4.cloned.1.call-update) | async-done | bytes 7864336 | tf_op jit(solution)/shard_map/all_gather | solution.py:46
  897.5 8.5 fusion.25
  906.2 1.0 reshape_broadcast_in_dim_reshape.6
  907.2 0.4 copy.68
  907.6 0.9 copy.69
  908.5 7.4 all-to-all-start.1
  916.1 1.0 gather_fusion
  917.8 9.2 fusion.22
  927.0 4.3 all-to-all-done.1
  931.3 1.1 copy.70
  932.4 0.5 copy.71
  932.9 0.9 squeeze_reshape.6
  933.8 0.8 fusion.39
  934.6 0.7 copy-done.2
  935.3 1.1 reshape_broadcast_in_dim.3
  936.5 0.4 copy.76
  936.9 0.2 copy.77
  937.1 27.6 %all_to_all.20 = f32[1,128,576]{2,0,1:T(1,128)S(1)} all-to-all(f32[1,128,576]{2,0,1:T(1,128)S(1)} %copy.77), channel_id=1, replica_groups=mesh['root'=4,'col'=128] {'col'}, dimensions={1} | all-to-all | bytes 589824 | tf_op jit(solution)/shard_map/all_to_all | solution.py:39
  964.7 0.2 copy.78
  964.9 0.5 copy.79
  965.3 0.9 reshape_squeeze_reshape.7
  966.3 1.0 gather_fusion.3
  967.4 8.6 fusion.31
  976.0 1.0 reshape_broadcast_in_dim_reshape.7
  977.0 0.4 copy.83
  977.4 0.9 copy.84
  978.4 8.1 all-to-all-start.3
  986.5 0.3 all-gather.6.cloned.1.call-start
  986.9 1.0 gather_fusion.2
  987.9 9.2 fusion.28
  997.1 4.9 all-to-all-done.3
  1002.0 1.1 copy.85
  1003.1 0.5 copy.86
  1003.6 0.9 squeeze_reshape.7
  1004.5 0.8 fusion.36
  1005.3 148.2 %all-gather.6.cloned.1.call-done = f32[96,3072]{1,0:T(8,128)} async-done(((f32[24,3072]{1,0:T(8,128)}), f32[96,3072]{1,0:T(8,128)}) %all-gather.6.cloned.1.call-update) | async-done | bytes 1179664 | tf_op jit(solution)/shard_map/all_gather | solution.py:59
  1153.6 3.9 fusion.20
  1157.5 0.8 copy.92
  (35 shorter events, 0.8 us)
Async XLA Ops:
  6.5 1147.0 %copy-start = (f32[4,4]{1,0:T(4,128)S(1)}, f32[4,4]{1,0:T(4,128)}, u32[]{:S(2)}) copy-start(f32[4,4]{1,0:T(4,128)} %param.11) | copy-start | bytes 196
  6.5 24.6 %copy-start.9 = (s32[24,10]{0,1:T(8,128)S(1)}, s32[24,10]{0,1:T(8,128)}, u32[]{:S(2)}) copy-start(s32[24,10]{0,1:T(8,128)} %param.13) | copy-start | bytes 2884
  6.5 891.0 %all-gather.4.cloned.1.call-start = ((), (), s32[]{:S(2)}) async-start(), calls=%async_computation.4 | async-start | bytes 7925760 | tf_op jit(solution)/shard_map/all_gather | solution.py:46
  10.8 42.2 %all-to-all-start = ((f32[1,128,576]{2,0,1:T(1,128)}), f32[1,128,576]{2,0,1:T(1,128)S(1)}, u32[]{:S(2)}, u32[]{:S(2)}) async-start(f32[1,128,576]{2,0,1:T(1,128)} %copy.62), calls=%async_computation | async-start | bytes 655360 | tf_op jit(solution)/shard_map/all_to_all | solution.py:39
  906.1 9.9 copy-start.1
  908.5 22.7 %all-to-all-start.1 = ((f32[1,128,576]{2,0,1:T(1,128)}), f32[1,128,576]{2,0,1:T(1,128)}, u32[]{:S(2)}, u32[]{:S(2)}) async-start(f32[1,128,576]{2,0,1:T(1,128)} %copy.69), calls=%async_computation.1 | async-start | bytes 655360 | tf_op jit(solution)/shard_map/all_to_all | solution.py:39
  927.0 6.8 copy-start.5
  927.0 6.8 copy-start.7
  934.6 0.7 copy-start.2
  975.9 10.9 copy-start.6
  978.4 23.7 %all-to-all-start.3 = ((f32[1,128,576]{2,0,1:T(1,128)}), f32[1,128,576]{2,0,1:T(1,128)}, u32[]{:S(2)}, u32[]{:S(2)}) async-start(f32[1,128,576]{2,0,1:T(1,128)} %copy.84), calls=%async_computation.3 | async-start | bytes 655360 | tf_op jit(solution)/shard_map/all_to_all | solution.py:39
  986.5 167.0 %all-gather.6.cloned.1.call-start = ((), (), s32[]{:S(2)}) async-start(), calls=%async_computation.5 | async-start | bytes 1474560 | tf_op jit(solution)/shard_map/all_gather | solution.py:59
  997.1 7.4 copy-start.3
  997.1 7.4 copy-start.4
  997.1 7.4 copy-start.8
Sparse Core Ops, SparseCore 0:
  9.4 888.0 all-gather.3
  1005.5 148.0 all-gather.5
where the time goes:
time: 1170 us
  waiting for transfers between devices  1020 us (87%)
  matrix products  39.5 us (3%)
  starting transfers between devices  36.2 us (3%)
  blocking collectives  27.6 us (2%)
  local copies, waits for them, and re-layouts  24.3 us (2%)
  between operations  14.3 us (1%)
    all_gather x1, waiting for transfers between devices, shards(): operator_blocks = lax.all_gather(string_blocks, 'col', axis=0, tiled=True)  842 us
    all_gather x1, waiting for transfers between devices, shards(): all_roots = lax.all_gather(second[None], 'root', axis=0, tiled=True)  148 us
    all_to_all x3, starting transfers between devices, swap_layout(): lax.all_to_all(layout_pieces(stacked), 'col', split_axis=1, concat_axis=1...  35.9 us
    dot_general x4, matrix products, apply_blocks(): jnp.einsum('rifk,ifjk->rij', picked, tiles, precision=lax.Precision.HIGHEST)  35.6 us
    all_to_all x3, waiting for transfers between devices, swap_layout(): lax.all_to_all(layout_pieces(stacked), 'col', split_axis=1, concat_axis=1...  30.6 us
    all_to_all x1, blocking collectives, swap_layout(): lax.all_to_all(layout_pieces(stacked), 'col', split_axis=1, concat_axis=1...  27.6 us
  transfers between devices with their start and end apart: 5, of which 5 were waited for; matrix products, arithmetic and copies ran while one was open for 2% of the time, Pallas kernels for 0%

commit v1 on v0

--- a/solution.py
+++ b/solution.py
@@ -43,7 +43,9 @@
 def shards(coeffs, diagonal, shift, rotation, string_blocks, block_cols):
     start = coeffs[0]
     energy = shift[0]
-    operator_blocks = lax.all_gather(string_blocks, "col", axis=0, tiled=True)
+    operator_blocks = jnp.concatenate(
+        lax.all_to_all(jnp.stack([string_blocks] * lax.axis_size("col")), "col", 0, 0), axis=0
+    )
 
     def apply_local(matrix):
         return apply_blocks(matrix, operator_blocks, block_cols)

time: 1170 us -> 598 us (0.51)
  waiting for transfers between devices: 1020 us -> 411 us
  blocking collectives: 27.6 us -> 72.1 us
    all_gather x1 -> x0, waiting for transfers between devices: 842 us -> none  [shards(): operator_blocks = lax.all_gather(string_blocks, 'col', axis=0, tiled=True)]
    all_to_all x0 -> x1, waiting for transfers between devices: none -> 339 us  [shards(): lax.all_to_all(jnp.stack([string_blocks] * lax.axis_size('col')), 'col',...]
    all_gather x1, waiting for transfers between devices: 148 us -> 51.5 us  [shards(): all_roots = lax.all_gather(second[None], 'root', axis=0, tiled=True)]
    all_to_all x1 -> x2, blocking collectives: 27.6 us -> 72.1 us  [swap_layout(): lax.all_to_all(layout_pieces(stacked), 'col', split_axis=1, concat_axis=1...]
    all_to_all x3 -> x2, starting transfers between devices: 35.9 us -> 21.1 us  [swap_layout(): lax.all_to_all(layout_pieces(stacked), 'col', split_axis=1, concat_axis=1...]
    all_to_all x3 -> x2, waiting for transfers between devices: 30.6 us -> 21.1 us  [swap_layout(): lax.all_to_all(layout_pieces(stacked), 'col', split_axis=1, concat_axis=1...]
  transfers between devices with their start and end apart: 5 -> 4, of which waited for: 5 -> 4; matrix products, arithmetic and copies ran while one was open for 2% -> 4% of each run, Pallas kernels for 0% -> 0%
where the time goes in v1:
time: 598 us; the launch traced here: 597 us
  waiting for transfers between devices  411 us (69%)
  blocking collectives  72.1 us (12%)
  matrix products  39.5 us (7%)
  starting transfers between devices  30.6 us (5%)
  local copies, waits for them, and re-layouts  27.8 us (5%)
  between operations  14.3 us (2%)
    all_to_all x1, waiting for transfers between devices, shards(): lax.all_to_all(jnp.stack([string_blocks] * lax.axis_size('col')), 'col',...  339 us
    all_to_all x2, blocking collectives, swap_layout(): lax.all_to_all(layout_pieces(stacked), 'col', split_axis=1, concat_axis=1...  72.1 us
    all_gather x1, waiting for transfers between devices, shards(): all_roots = lax.all_gather(second[None], 'root', axis=0, tiled=True)  51.5 us
    dot_general x4, matrix products, apply_blocks(): jnp.einsum('rifk,ifjk->rij', picked, tiles, precision=lax.Precision.HIGHEST)  35.6 us
    all_to_all x2, waiting for transfers between devices, swap_layout(): lax.all_to_all(layout_pieces(stacked), 'col', split_axis=1, concat_axis=1...  21.1 us
    all_to_all x2, starting transfers between devices, swap_layout(): lax.all_to_all(layout_pieces(stacked), 'col', split_axis=1, concat_axis=1...  21.1 us
  transfers between devices with their start and end apart: 4, of which 4 were waited for; matrix products, arithmetic and copies ran while one was open for 4% of the time, Pallas kernels for 0%

profile of v1, /device:TPU:1, one launch (start us, length us, event | category | flops | bytes accessed | tf_op | source)
XLA Modules:
  0.0 597.1 jit_solution(15304999667335352467)
XLA Ops:
  6.5 2.1 reshape_broadcast_in_dim_squeeze.3
  8.7 0.4 copy.61
  9.1 0.2 copy.62
  9.3 42.0 %all_to_all.25 = f32[1,128,576]{2,0,1:T(1,128)S(1)} all-to-all(f32[1,128,576]{2,0,1:T(1,128)S(1)} %copy.62), channel_id=1, replica_groups=mesh['root'=4,'col'=128] {'col'}, dimensions={1} | all-to-all | bytes 589824 | tf_op jit(solution)/shard_map/all_to_all | solution.py:39
  51.3 4.2 stack.2
  55.5 9.2 %all-to-all-start = ((bf16[128,240,128]{2,1,0:T(8,128)(2,1)}), bf16[128,240,128]{2,1,0:T(8,128)(2,1)}, u32[]{:S(2)}, u32[]{:S(2)}) async-start(bf16[128,240,128]{2,1,0:T(8,128)(2,1)} %stack.2), calls=%async_computation | async-start | bytes 15728640 | tf_op jit(solution)/shard_map/all_to_all | solution.py:47
  65.0 0.2 copy.63
  65.2 0.5 copy.64
  65.7 0.9 reshape_squeeze_reshape.6
  66.7 1.0 gather_fusion.1
  67.7 338.6 %all-to-all-done = bf16[128,240,128]{2,1,0:T(8,128)(2,1)} async-done(((bf16[128,240,128]{2,1,0:T(8,128)(2,1)}), bf16[128,240,128]{2,1,0:T(8,128)(2,1)}, u32[]{:S(2)}, u32[]{:S(2)}) %all-to-all-start) | async-done | bytes 7864352 | tf_op jit(solution)/shard_map/all_to_all | solution.py:47
  406.3 8.5 %fusion.25 = f32[24,24,128]{2,0,1:T(8,128)S(1)} fusion(bf16[24,10,128,128]{3,2,1,0:T(8,128)(2,1)} %bitcast.4, f32[24,10,24,128]{3,2,1,0:T(8,128)S(1)} %bitcast.122, pred[24,10]{1,0:T(8,128)(4,1)S(1)} %copy.55), kind=kOutput, calls=%fused_computation.27 | convolution fusion | flops 1133199360 | bytes 11108592 | tf_op jit(solution)/shard_map/rifk,ifjk->rij/dot_general | solution.py:14
  414.9 1.0 reshape_broadcast_in_dim_reshape.6
  415.9 0.4 copy.68
  416.4 1.0 copy.69
  417.3 12.0 %all-to-all-start.2 = ((f32[1,128,576]{2,0,1:T(1,128)}), f32[1,128,576]{2,0,1:T(1,128)}, u32[]{:S(2)}, u32[]{:S(2)}) async-start(f32[1,128,576]{2,0,1:T(1,128)} %copy.69), calls=%async_computation.2 | async-start | bytes 655360 | tf_op jit(solution)/shard_map/all_to_all | solution.py:39
  429.4 1.0 gather_fusion
  431.1 9.2 %fusion.22 = f32[24,3,8,128]{3,2,1,0:T(8,128)} fusion(bf16[24,10,128,128]{3,2,1,0:T(8,128)(2,1)} %bitcast.4, f32[24,10,24,128]{3,2,1,0:T(8,128)S(1)} %bitcast.124, pred[24,10]{1,0:T(8,128)(4,1)S(1)} %copy.55), kind=kOutput, calls=%fused_computation.26 | convolution fusion | flops 1133199360 | bytes 11108592 | tf_op jit(solution)/shard_map/rifk,ifjk->rij/dot_general | solution.py:14
  440.3 10.4 %all-to-all-done.2 = f32[1,128,576]{2,0,1:T(1,128)} async-done(((f32[1,128,576]{2,0,1:T(1,128)}), f32[1,128,576]{2,0,1:T(1,128)}, u32[]{:S(2)}, u32[]{:S(2)}) %all-to-all-start.2) | async-done | bytes 294944 | tf_op jit(solution)/shard_map/all_to_all | solution.py:39
  450.7 1.1 copy.70
  451.8 0.5 copy.71
  452.3 0.9 squeeze_reshape.6
  453.2 0.8 fusion.39
  453.9 0.7 copy-done.2
  454.7 1.1 reshape_broadcast_in_dim.3
  455.8 0.4 copy.76
  456.3 0.2 copy.77
  456.5 30.1 %all_to_all.26 = f32[1,128,576]{2,0,1:T(1,128)S(1)} all-to-all(f32[1,128,576]{2,0,1:T(1,128)S(1)} %copy.77), channel_id=1, replica_groups=mesh['root'=4,'col'=128] {'col'}, dimensions={1} | all-to-all | bytes 589824 | tf_op jit(solution)/shard_map/all_to_all | solution.py:39
  486.6 0.2 copy.78
  486.8 0.5 copy.79
  487.3 0.9 reshape_squeeze_reshape.7
  488.3 1.0 gather_fusion.3
  489.3 8.6 %fusion.31 = f32[24,24,128]{2,0,1:T(8,128)S(1)} fusion(bf16[24,10,128,128]{3,2,1,0:T(8,128)(2,1)} %bitcast.4, f32[24,10,24,128]{3,2,1,0:T(8,128)S(1)} %bitcast.125, pred[24,10]{1,0:T(8,128)(4,1)S(1)} %copy.55), kind=kOutput, calls=%fused_computation.29 | convolution fusion | flops 1133199360 | bytes 11108592 | tf_op jit(solution)/shard_map/rifk,ifjk->rij/dot_general | solution.py:14
  497.9 1.0 reshape_broadcast_in_dim_reshape.7
  498.9 0.4 copy.83
  499.3 1.0 copy.84
  500.3 9.1 %all-to-all-start.4 = ((f32[1,128,576]{2,0,1:T(1,128)}), f32[1,128,576]{2,0,1:T(1,128)}, u32[]{:S(2)}, u32[]{:S(2)}) async-start(f32[1,128,576]{2,0,1:T(1,128)} %copy.84), calls=%async_computation.4 | async-start | bytes 655360 | tf_op jit(solution)/shard_map/all_to_all | solution.py:39
  509.4 0.3 all-gather.3.cloned.1.call-start
  509.7 1.0 gather_fusion.2
  510.8 9.2 %fusion.28 = f32[24,3,8,128]{3,2,1,0:T(8,128)} fusion(bf16[24,10,128,128]{3,2,1,0:T(8,128)(2,1)} %bitcast.4, f32[24,10,24,128]{3,2,1,0:T(8,128)S(1)} %bitcast.123, pred[24,10]{1,0:T(8,128)(4,1)S(1)} %copy.55), kind=kOutput, calls=%fused_computation.28 | convolution fusion | flops 1133199360 | bytes 11108592 | tf_op jit(solution)/shard_map/rifk,ifjk->rij/dot_general | solution.py:14
  520.0 10.7 %all-to-all-done.4 = f32[1,128,576]{2,0,1:T(1,128)} async-done(((f32[1,128,576]{2,0,1:T(1,128)}), f32[1,128,576]{2,0,1:T(1,128)}, u32[]{:S(2)}, u32[]{:S(2)}) %all-to-all-start.4) | async-done | bytes 294944 | tf_op jit(solution)/shard_map/all_to_all | solution.py:39
  530.7 1.1 copy.85
  531.8 0.5 copy.86
  532.3 0.9 squeeze_reshape.7
  533.2 0.8 fusion.36
  534.0 51.5 %all-gather.3.cloned.1.call-done = f32[96,3072]{1,0:T(8,128)} async-done(((f32[24,3072]{1,0:T(8,128)}), f32[96,3072]{1,0:T(8,128)}) %all-gather.3.cloned.1.call-update) | async-done | bytes 1179664 | tf_op jit(solution)/shard_map/all_gather | solution.py:61
  585.6 3.9 fusion.20
  589.5 0.8 copy.92
  (36 shorter events, 0.8 us)
Async XLA Ops:
  6.5 579.0 %copy-start = (f32[4,4]{1,0:T(4,128)S(1)}, f32[4,4]{1,0:T(4,128)}, u32[]{:S(2)}) copy-start(f32[4,4]{1,0:T(4,128)} %param.11) | copy-start | bytes 196
  6.5 44.8 %copy-start.9 = (bf16[240,128]{1,0:T(8,128)(2,1)S(1)}, bf16[240,128]{1,0:T(8,128)(2,1)}, u32[]{:S(2)}) copy-start(bf16[240,128]{1,0:T(8,128)(2,1)} %param.12) | copy-start | bytes 184324
  55.5 9.2 %copy-start.10 = (s32[24,10]{0,1:T(8,128)S(1)}, s32[24,10]{0,1:T(8,128)}, u32[]{:S(2)}) copy-start(s32[24,10]{0,1:T(8,128)} %param.13) | copy-start | bytes 2884
  55.5 350.8 %all-to-all-start = ((bf16[128,240,128]{2,1,0:T(8,128)(2,1)}), bf16[128,240,128]{2,1,0:T(8,128)(2,1)}, u32[]{:S(2)}, u32[]{:S(2)}) async-start(bf16[128,240,128]{2,1,0:T(8,128)(2,1)} %stack.2), calls=%async_computation | async-start | bytes 15728640 | tf_op jit(solution)/shard_map/all_to_all | solution.py:47
  414.8 14.4 %copy-start.1 = (f32[1,24,3072]{2,1,0:T(8,128)S(1)}, f32[1,24,3072]{2,1,0:T(8,128)}, u32[]{:S(2)}) copy-start(f32[1,24,3072]{2,1,0:T(8,128)} %param.8) | copy-start | bytes 884740
  417.3 33.4 %all-to-all-start.2 = ((f32[1,128,576]{2,0,1:T(1,128)}), f32[1,128,576]{2,0,1:T(1,128)}, u32[]{:S(2)}, u32[]{:S(2)}) async-start(f32[1,128,576]{2,0,1:T(1,128)} %copy.69), calls=%async_computation.2 | async-start | bytes 655360 | tf_op jit(solution)/shard_map/all_to_all | solution.py:39
  440.3 12.8 %copy-start.5 = (f32[24,3,8,128]{3,2,1,0:T(8,128)S(1)}, f32[24,3,8,128]{3,2,1,0:T(8,128)}, u32[]{:S(2)}) copy-start(f32[24,3,8,128]{3,2,1,0:T(8,128)} %fusion.22) | copy-start | bytes 884740
  440.3 12.8 %copy-start.7 = (f32[24,3072]{1,0:T(8,128)S(1)}, f32[24,3072]{1,0:T(8,128)}, u32[]{:S(2)}) copy-start(f32[24,3072]{1,0:T(8,128)} %param.9) | copy-start | bytes 884740
  453.9 0.7 copy-start.2
  497.8 11.9 %copy-start.6 = (f32[3,24,8,128]{3,2,1,0:T(8,128)S(1)}, f32[3,24,8,128]{3,2,1,0:T(8,128)}, u32[]{:S(2)}) copy-start(f32[3,24,8,128]{3,2,1,0:T(8,128)} %get-tuple-element.6) | copy-start | bytes 884740
  500.3 30.4 %all-to-all-start.4 = ((f32[1,128,576]{2,0,1:T(1,128)}), f32[1,128,576]{2,0,1:T(1,128)}, u32[]{:S(2)}, u32[]{:S(2)}) async-start(f32[1,128,576]{2,0,1:T(1,128)} %copy.84), calls=%async_computation.4 | async-start | bytes 655360 | tf_op jit(solution)/shard_map/all_to_all | solution.py:39
  509.4 76.2 %all-gather.3.cloned.1.call-start = ((), (), s32[]{:S(2)}) async-start(), calls=%async_computation.5 | async-start | bytes 1474560 | tf_op jit(solution)/shard_map/all_gather | solution.py:61
  520.0 13.2 %copy-start.3 = (f32[24,3072]{1,0:T(8,128)S(1)}, f32[24,3072]{1,0:T(8,128)}, u32[]{:S(2)}) copy-start(f32[24,3072]{1,0:T(8,128)} %copy-done.2) | copy-start | bytes 884740
  520.0 13.2 %copy-start.4 = (f32[24,3,8,128]{3,2,1,0:T(8,128)S(1)}, f32[24,3,8,128]{3,2,1,0:T(8,128)}, u32[]{:S(2)}) copy-start(f32[24,3,8,128]{3,2,1,0:T(8,128)} %fusion.28) | copy-start | bytes 884740
  520.0 13.2 %copy-start.8 = (f32[24,3072]{1,0:T(8,128)S(1)}, f32[24,3072]{1,0:T(8,128)}, u32[]{:S(2)}) copy-start(f32[24,3072]{1,0:T(8,128)} %param.9) | copy-start | bytes 884740
Sparse Core Ops, SparseCore 0:
  534.2 51.3 all-gather.2
